TPU v7x, 32 devices: a whole 2x2x4 slice. The times are simulated.
32 devices in a mesh: fsdp: 16 (over z, y, core), tp: 2 (over x).
Axes of the slice: x: 2, y: 2, z: 4, core: 2. Of those that a mesh axis runs over, the one named last changes fastest.
Arguments:
- tokens: bfloat16 [16, 1024, 1152], P('fsdp', 'tp'), may hold values from -6 to 6
- condition: bfloat16 [16, 1152], P('fsdp'), may hold values from -3 to 3
- mod_weight: bfloat16 [1152, 6912], P('tp', 'fsdp'), may hold values from -0.088388348 to 0.088388348
- mod_bias: bfloat16 [6912], P('fsdp'), may hold values from -1.5 to 1.5
- qkv_weight: bfloat16 [1152, 3, 1152], P('fsdp', None, 'tp'), may hold values from -0.088388348 to 0.088388348
- qv_bias: bfloat16 [2, 1152], P(None, 'fsdp'), may hold values from -2 to 2
- out_weight: bfloat16 [1152, 1152], P('tp', 'fsdp'), may hold values from -0.75 to 0.75
- out_bias: bfloat16 [1152], P('fsdp'), may hold values from -3 to 3
- up_weight: bfloat16 [1152, 4608], P('fsdp', 'tp'), may hold values from -0.1875 to 0.1875
- up_bias: bfloat16 [4608], P('fsdp'), may hold values from -3 to 3
- down_weight: bfloat16 [4608, 1152], P('tp', 'fsdp'), may hold values from -0.09375 to 0.09375
- down_bias: bfloat16 [1152], P('fsdp'), may hold values from -3 to 3
- cotangent: bfloat16 [16, 1024, 1152], P('fsdp', 'tp'), may hold values from -6 to 6
Outputs:
- result: bfloat16 [16, 1024, 1152], P('fsdp', 'tp')
- tokens_grad: bfloat16 [16, 1024, 1152], P('fsdp', 'tp')
- condition_grad: float32 [16, 1152], P('fsdp', 'tp')
- mod_weight_grad: float32 [1152, 6912], P('tp', 'fsdp')
- mod_bias_grad: float32 [6912], P('fsdp')
- qkv_weight_grad: float32 [1152, 3, 1152], P('fsdp', None, 'tp')
- qv_bias_grad: float32 [2, 1152], P(None, 'fsdp')
- out_weight_grad: float32 [1152, 1152], P('tp', 'fsdp')
- out_bias_grad: float32 [1152], P('fsdp')
- up_weight_grad: float32 [1152, 4608], P('fsdp', 'tp')
- up_bias_grad: float32 [4608], P('fsdp')
- down_weight_grad: float32 [4608, 1152], P('tp', 'fsdp')
- down_bias_grad: float32 [1152], P('fsdp')
All inputs are finite; a program needn't handle non-finite values.
Results may differ from a plain program's by a relative error of at most 0.015.
Values may be sent and summed in bfloat16 or wider, within the bound.
A program may use at most 256 MiB of HBM per device.

v0:
```python
import math
import jax
import jax.numpy as jnp
from jax import lax
from jax.sharding import PartitionSpec as P

HEAD_DIM = 72
EPSILON = 1e-06
HIGH = lax.Precision.HIGHEST


def normalize(values):
    center = values - jnp.mean(values, axis=-1, keepdims=True)
    variance = jnp.mean(center * center, axis=-1, keepdims=True)
    inverse = lax.rsqrt(variance + EPSILON)
    return (center * inverse, inverse)


def norm_back(grad_norm, normed, inverse):
    first_mean = jnp.mean(grad_norm, axis=-1, keepdims=True)
    second_mean = jnp.mean(grad_norm * normed, axis=-1, keepdims=True)
    return inverse * (grad_norm - first_mean - normed * second_mean)


def inner_rows(left, right):
    return lax.dot_general(
        left, right, (((0,), (0,)), ((), ())), preferred_element_type=jnp.float32
    )


def outer_cols(left, right):
    return lax.dot_general(
        left, right, (((1,), (1,)), ((), ())), preferred_element_type=jnp.float32
    )


def gelu_tanh(values):
    return jax.nn.gelu(values, approximate=True)


def to_heads(flat, head_count):
    return flat.reshape(flat.shape[0], head_count, HEAD_DIM).transpose(1, 0, 2)


def from_heads(stacked):
    return stacked.transpose(1, 0, 2).reshape(stacked.shape[1], stacked.shape[0] * HEAD_DIM)


def swap(values):
    return lax.ppermute(values, "tp", [(0, 1), (1, 0)])


def gather_rows(values, tp_count):
    if tp_count == 2:
        return jnp.concatenate([values, swap(values)], axis=0)
    return lax.all_gather(values, "tp", axis=0, tiled=True)


def scatter_rows(left, right, contract, tp_count):
    if tp_count == 2:
        half = left.shape[0] // 2
        sent = swap(contract(left[half:], right).astype(jnp.bfloat16))
        return contract(left[:half], right) + sent.astype(jnp.float32)
    return lax.psum_scatter(
        contract(left, right).astype(jnp.bfloat16), "tp", scatter_dimension=0, tiled=True
    ).astype(jnp.float32)


def sum_pair(values, tp_count):
    if tp_count == 2:
        return values + swap(values)
    return lax.psum(values, "tp")


def plain(left, right):
    return jnp.dot(left, right, preferred_element_type=jnp.float32)


def reduce_grad(term, axis):
    return lax.psum_scatter(term.astype(jnp.bfloat16), "fsdp", scatter_dimension=axis, tiled=True)


def gather_small(flat):
    size = flat.shape[0]
    padded = -(-size // 1024) * 1024
    block = jnp.pad(flat, (0, padded - size)).reshape(8, padded // 8)
    return lax.all_gather(block, "fsdp", axis=0, tiled=True).reshape(-1, padded)[:, :size]


def trade(rows):
    return lax.all_to_all(rows, "fsdp", split_axis=0, concat_axis=0, tiled=True)


def shards(
    tokens,
    condition,
    mod_weight,
    mod_bias,
    qkv_weight,
    qv_bias,
    out_weight,
    out_bias,
    up_weight,
    up_bias,
    down_weight,
    down_bias,
    cotangent,
):
    tp_count = lax.axis_size("tp")
    tp_place = lax.axis_index("tp")
    fsdp_count = lax.axis_size("fsdp")
    local_rows = tokens.shape[1]
    width = tokens.shape[2]
    seq_len = local_rows * tp_count
    share = width // tp_count
    thin = width // fsdp_count
    hidden_thin = up_bias.shape[0]
    hidden_full = hidden_thin * fsdp_count
    mod_thin = mod_bias.shape[0]
    small = gather_small(
        jnp.concatenate([condition[0], qv_bias.reshape(-1), out_bias, up_bias, down_bias])
    ).astype(jnp.float32)
    qkv_full = lax.all_gather(qkv_weight, "fsdp", axis=0, tiled=True)
    out_full = lax.all_gather(out_weight, "fsdp", axis=1, tiled=True)
    up_full = lax.all_gather(up_weight, "fsdp", axis=0, tiled=True)
    down_full = lax.all_gather(down_weight, "fsdp", axis=1, tiled=True)
    cond_all = small[:, :width]
    spot = width
    qv_full = (
        small[:, spot : spot + 2 * thin]
        .reshape(fsdp_count, 2, thin)
        .transpose(1, 0, 2)
        .reshape(2, width)
    )
    spot += 2 * thin
    out_shift = small[:, spot : spot + thin].reshape(-1)
    spot += thin
    up_shift = small[:, spot : spot + hidden_thin].reshape(-1)
    spot += hidden_thin
    down_shift = small[:, spot : spot + thin].reshape(-1)
    head_cols = qkv_full.shape[2]
    head_count = head_cols // HEAD_DIM
    hidden_cols = up_full.shape[1]
    cond_part = lax.dynamic_slice_in_dim(cond_all, tp_place * share, share, 1)
    silu_low = jax.nn.silu(cond_part).astype(jnp.bfloat16)
    partial_mod = jnp.dot(silu_low, mod_weight, preferred_element_type=jnp.float32)
    modulation = trade(sum_pair(partial_mod, tp_count) + mod_bias.astype(jnp.float32)).reshape(-1)
    pieces = modulation.reshape(6, width)
    shift_one = pieces[0]
    scale_one = pieces[1]
    gate_one = pieces[2]
    shift_two = pieces[3]
    scale_two = pieces[4]
    gate_two = pieces[5]
    rows_in = tokens[0].astype(jnp.float32)
    normed_one, inverse_one = normalize(rows_in)
    hidden_one = gather_rows(
        (normed_one * (1.0 + scale_one) + shift_one).astype(jnp.bfloat16), tp_count
    )
    qkv_matrix = qkv_full.reshape(width, 3 * head_cols)
    projected = plain(hidden_one, qkv_matrix).reshape(seq_len, 3, head_cols)
    qv_local = lax.dynamic_slice_in_dim(qv_full, tp_place * head_cols, head_cols, 1)
    queries = to_heads((projected[:, 0] + qv_local[0]).astype(jnp.bfloat16), head_count)
    keys_all = to_heads(projected[:, 1].astype(jnp.bfloat16), head_count)
    values_all = to_heads((projected[:, 2] + qv_local[1]).astype(jnp.bfloat16), head_count)
    grad_rows = cotangent[0].astype(jnp.float32)
    grad_two_own = (grad_rows * gate_two).astype(jnp.bfloat16)
    grad_branch_two = gather_rows(grad_two_own, tp_count)
    block = min(512, seq_len)
    block_count = seq_len // block
    scaling = 1.0 / math.sqrt(HEAD_DIM)
    query_blocks = queries.reshape(head_count, block_count, block, HEAD_DIM).transpose(1, 0, 2, 3)

    def attend(query_block):
        scores = (
            jnp.einsum("hqd,hkd->hqk", query_block, keys_all, preferred_element_type=jnp.float32)
            * scaling
        )
        highest = jnp.max(scores, axis=-1, keepdims=True)
        raised = jnp.exp(scores - highest)
        totals = jnp.sum(raised, axis=-1, keepdims=True)
        weights = (raised / totals).astype(jnp.bfloat16)
        output = jnp.einsum("hqk,hkd->hqd", weights, values_all, preferred_element_type=jnp.float32)
        return (output, (highest + jnp.log(totals))[..., 0])

    attended_blocks, log_totals = lax.map(attend, query_blocks)
    attended = attended_blocks.transpose(1, 0, 2, 3).reshape(head_count, seq_len, HEAD_DIM)
    attended_low = from_heads(attended).astype(jnp.bfloat16)
    branch_one = scatter_rows(attended_low, out_full, plain, tp_count) + out_shift
    middle = rows_in + gate_one * branch_one
    normed_two, inverse_two = normalize(middle)
    hidden_two = gather_rows(
        (normed_two * (1.0 + scale_two) + shift_two).astype(jnp.bfloat16), tp_count
    )
    up_local = lax.dynamic_slice_in_dim(up_shift, tp_place * hidden_cols, hidden_cols)
    before = plain(hidden_two, up_full) + up_local
    activated, gelu_pull = jax.vjp(gelu_tanh, before)
    activated_low = activated.astype(jnp.bfloat16)
    grad_before = gelu_pull(outer_cols(grad_branch_two, down_full))[0].astype(jnp.bfloat16)
    grad_hidden_two = scatter_rows(grad_before, up_full, outer_cols, tp_count)
    branch_two = scatter_rows(activated_low, down_full, plain, tp_count) + down_shift
    outcome = (middle + gate_two * branch_two).astype(jnp.bfloat16)
    grad_gate_two = jnp.sum(grad_rows * branch_two, axis=0)
    down_bias_part = jnp.sum(grad_two_own.astype(jnp.float32), axis=0)
    down_grad = reduce_grad(inner_rows(activated_low, grad_branch_two), 1)
    up_bias_part = jnp.sum(grad_before.astype(jnp.float32), axis=0)
    up_grad = reduce_grad(inner_rows(hidden_two, grad_before), 0)
    grad_scale_two = jnp.sum(grad_hidden_two * normed_two, axis=0)
    grad_shift_two = jnp.sum(grad_hidden_two, axis=0)
    grad_middle = grad_rows + norm_back(
        grad_hidden_two * (1.0 + scale_two), normed_two, inverse_two
    )
    grad_gate_one = jnp.sum(grad_middle * branch_one, axis=0)
    grad_one_own = (grad_middle * gate_one).astype(jnp.bfloat16)
    grad_branch_one = gather_rows(grad_one_own, tp_count)
    out_bias_part = jnp.sum(grad_one_own.astype(jnp.float32), axis=0)
    out_grad = reduce_grad(inner_rows(attended_low, grad_branch_one), 1)
    grad_attended = outer_cols(grad_branch_one, out_full).astype(jnp.bfloat16)
    grad_blocks = (
        to_heads(grad_attended, head_count)
        .reshape(head_count, block_count, block, HEAD_DIM)
        .transpose(1, 0, 2, 3)
    )

    def attend_back(carry, inputs):
        grad_keys, grad_values = carry
        query_block, log_block, grad_block = inputs
        scores = (
            jnp.einsum("hqd,hkd->hqk", query_block, keys_all, preferred_element_type=jnp.float32)
            * scaling
        )
        weights = jnp.exp(scores - log_block[..., None])
        grad_weights = jnp.einsum(
            "hqd,hkd->hqk", grad_block, values_all, preferred_element_type=jnp.float32
        )
        centered = jnp.sum(weights * grad_weights, axis=-1, keepdims=True)
        grad_scores = (weights * (grad_weights - centered)).astype(jnp.bfloat16)
        grad_query = (
            jnp.einsum("hqk,hkd->hqd", grad_scores, keys_all, preferred_element_type=jnp.float32)
            * scaling
        )
        grad_keys = (
            grad_keys
            + jnp.einsum(
                "hqk,hqd->hkd", grad_scores, query_block, preferred_element_type=jnp.float32
            )
            * scaling
        )
        grad_values = grad_values + jnp.einsum(
            "hqk,hqd->hkd",
            weights.astype(jnp.bfloat16),
            grad_block,
            preferred_element_type=jnp.float32,
        )
        return ((grad_keys, grad_values), grad_query)

    zero_heads = jnp.zeros((head_count, seq_len, HEAD_DIM), jnp.float32)
    (grad_keys, grad_values), grad_query_blocks = lax.scan(
        attend_back, (zero_heads, zero_heads), (query_blocks, log_totals, grad_blocks)
    )
    grad_queries = grad_query_blocks.transpose(1, 0, 2, 3).reshape(head_count, seq_len, HEAD_DIM)
    grad_projected = jnp.stack(
        [from_heads(grad_queries), from_heads(grad_keys), from_heads(grad_values)], axis=1
    ).astype(jnp.bfloat16)
    grad_projected, down_grad, up_grad, out_grad = lax.optimization_barrier(
        (grad_projected, down_grad, up_grad, out_grad)
    )
    qv_bias_part = jnp.sum(grad_projected[:, 0::2].astype(jnp.float32), axis=0)
    grad_flat = grad_projected.reshape(seq_len, 3 * head_cols)
    grad_hidden_one = scatter_rows(grad_flat, qkv_matrix, outer_cols, tp_count)
    qkv_grad = reduce_grad(inner_rows(hidden_one, grad_flat).reshape(width, 3, head_cols), 0)
    grad_scale_one = jnp.sum(grad_hidden_one * normed_one, axis=0)
    grad_shift_one = jnp.sum(grad_hidden_one, axis=0)
    grad_tokens = grad_middle + norm_back(
        grad_hidden_one * (1.0 + scale_one), normed_one, inverse_one
    )
    grad_mod_part = jnp.concatenate(
        [
            grad_shift_one,
            grad_scale_one,
            grad_gate_one,
            grad_shift_two,
            grad_scale_two,
            grad_gate_two,
        ]
    )
    qv_padded = lax.dynamic_update_slice_in_dim(
        jnp.zeros((2, width), jnp.float32), qv_bias_part, tp_place * head_cols, 1
    )
    up_padded = lax.dynamic_update_slice_in_dim(
        jnp.zeros((hidden_full,), jnp.float32), up_bias_part, tp_place * hidden_cols, 0
    )
    packed = jnp.concatenate(
        [
            grad_mod_part.reshape(fsdp_count, mod_thin),
            qv_padded.reshape(2, fsdp_count, thin).transpose(1, 0, 2).reshape(fsdp_count, 2 * thin),
            out_bias_part.reshape(fsdp_count, thin),
            up_padded.reshape(fsdp_count, hidden_thin),
            down_bias_part.reshape(fsdp_count, thin),
        ],
        axis=1,
    )
    traded = sum_pair(trade(packed), tp_count)
    totals = jnp.sum(traded, axis=0)
    grad_mod = traded[:, :mod_thin]
    mod_weight_grad = lax.dot_general(
        silu_low.astype(jnp.float32), grad_mod, (((0,), (0,)), ((), ())), precision=HIGH
    )
    silu_parts = lax.dot_general(
        grad_mod, mod_weight.astype(jnp.float32), (((1,), (1,)), ((), ())), precision=HIGH
    )
    grad_silu = jnp.sum(trade(silu_parts), axis=0)
    cond_row = condition[0].astype(jnp.float32)
    own_part = lax.dynamic_slice_in_dim(cond_row, tp_place * share, share)
    cond_grad = jax.vjp(jax.nn.silu, own_part)[1](grad_silu)[0][None, :]
    spot = mod_thin
    qv_bias_grad = totals[spot : spot + 2 * thin].reshape(2, thin)
    spot += 2 * thin
    out_bias_grad = totals[spot : spot + thin]
    spot += thin
    up_bias_grad = totals[spot : spot + hidden_thin]
    spot += hidden_thin
    down_bias_grad = totals[spot : spot + thin]
    return (
        outcome[None],
        grad_tokens.astype(jnp.bfloat16)[None],
        cond_grad,
        mod_weight_grad,
        totals[:mod_thin],
        qkv_grad.astype(jnp.float32),
        qv_bias_grad,
        out_grad.astype(jnp.float32),
        out_bias_grad,
        up_grad.astype(jnp.float32),
        up_bias_grad,
        down_grad.astype(jnp.float32),
        down_bias_grad,
    )


def solution(mesh):
    return jax.shard_map(
        shards,
        mesh=mesh,
        in_specs=(
            P("fsdp", "tp", None),
            P("fsdp", None),
            P("tp", "fsdp"),
            P("fsdp"),
            P("fsdp", None, "tp"),
            P(None, "fsdp"),
            P("tp", "fsdp"),
            P("fsdp"),
            P("fsdp", "tp"),
            P("fsdp"),
            P("tp", "fsdp"),
            P("fsdp"),
            P("fsdp", "tp", None),
        ),
        out_specs=(
            P("fsdp", "tp", None),
            P("fsdp", "tp", None),
            P("fsdp", "tp"),
            P("tp", "fsdp"),
            P("fsdp"),
            P("fsdp", None, "tp"),
            P(None, "fsdp"),
            P("tp", "fsdp"),
            P("fsdp"),
            P("fsdp", "tp"),
            P("fsdp"),
            P("tp", "fsdp"),
            P("fsdp"),
        ),
        check_vma=False,
    )
```

profile of v0, /device:TPU:0, one launch (start us, length us, event | category | flops | bytes accessed | tf_op | source)
XLA Modules:
  0.0 673.1 jit_solution(11910449368759546914)
XLA Ops:
  13.0 23.3 %all_gather.15 = bf16[128,256]{1,0:T(8,128)(2,1)S(1)} all-gather(bf16[8,256]{1,0:T(8,128)(2,1)S(1)} %reshape.202), channel_id=1, replica_groups=mesh['fsdp'=16,'tp'=2] {'fsdp'}, dimensions={0}, use_global_device_ids=true | all-gather | bytes 69632 | tf_op jit(solution)/shard_map/all_gather | solution.py:87
  55.5 9.6 %all-gather.5.cloned.1.call-done = bf16[1152,3,576]{2,0,1:T(8,128)(2,1)} async-done(((bf16[72,3,576]{2,0,1:T(8,128)(2,1)}), bf16[1152,3,576]{2,0,1:T(8,128)(2,1)}) %all-gather.5.cloned.1.call-update) | async-done | bytes 3981328 | tf_op jit(solution)/shard_map/all_gather | solution.py:123
  96.9 23.9 %while.27 = (s32[]{:T(128)}, bf16[2,8,512,72]{2,3,1,0:T(8,128)(2,1)}, f32[2,8,512]{2,1,0:T(8,128)S(1)}, bf16[2,8,512,72]{2,3,1,0:T(8,128)(2,1)S(1)}, bf16[8,1024...) while((s32[]{:T(128)}, bf16[2,8,512,72]{2,3,1,0:T(8,128)(2,1)}, ...), condition=%wide.region_5.6_spmd, body=%wide.region_2.5_spmd.sunk | while | flops 1245704192 | bytes 68747440 | solution.py:186
  131.7 23.0 %collective-permute-done.2 = bf16[512,1152]{1,0:T(8,128)(2,1)} collective-permute-done((bf16[512,1152]{1,0:T(8,128)(2,1)}, bf16[512,1152]{1,0:T(8,128)(2,1)}, u32[]{:S(2)}, u32[]{:S(2)}) %collective-permute-start.2) | collective-permute-done | bytes 1179680 | tf_op jit(solution)/shard_map/ppermute | solution.py:50
  168.1 22.9 %collective-permute-done.3 = bf16[512,1152]{1,0:T(8,128)(2,1)} collective-permute-done((bf16[512,1152]{1,0:T(8,128)(2,1)}, bf16[512,1152]{1,0:T(8,128)(2,1)}, u32[]{:S(2)}, u32[]{:S(2)}) %collective-permute-start.3) | collective-permute-done | bytes 1179680 | tf_op jit(solution)/shard_map/ppermute | solution.py:50
  191.0 14.7 %multiply_convert_fusion.1 = (bf16[1024,2304]{1,0:T(8,128)(2,1)}, f32[1024,2304]{1,0:T(8,128)}) fusion(f32[2304]{0:T(1024)S(1)} %dynamic_slice.28, bf16[1152,2304]{1,0:T(8,128)(2,1)} %all-gather.9.cloned.1.call-done, bf16[512,1152]{1,0:T(8,128)(2,1)} %collective-permute-done.3, bf16[512,1152]{1,0:T(8,128)(2,1)} %add_convert_fusion.1), kind=kOutput, calls=%fused_computation.53 | convolution fusion | flops 5464129536 | bytes 21832704 | tf_op jit(solution)/shard_map/dot_general | solution.py:76
  219.6 17.0 %convert_reduce_fusion = (f32[2304]{0:T(1024)}, bf16[1024,2304]{1,0:T(8,128)(2,1)}) fusion(f32[1024,2304]{1,0:T(8,128)} %get-tuple-element.259, f32[2304]{0:T(1024)S(1)} %dynamic_slice.28, bf16[2304,1152]{0,1:T(8,128)(2,1)} %all-gather.11.cloned.1.call-done, bf16[512,1152]{1,0:T(8,128)(2,1)} %collective-permute-done.5, bf16[512,1152]{1,0:T(8,128)(2,1)} %get-tuple-element.232), kind=kOutput, calls=%fused_computation.52 | convolution fusion | flops 5494798336 | bytes 21841920 | tf_op jit(solution)/shard_map/dot_general | solution.py:32
  252.1 18.5 %collective-permute-done.6 = bf16[512,1152]{1,0:T(8,128)(2,1)S(1)} collective-permute-done((bf16[512,1152]{1,0:T(8,128)(2,1)S(1)}, bf16[512,1152]{1,0:T(8,128)(2,1)S(1)}, u32[]{:S(2)}, u32[]{:S(2)}) %collective-permute-start.6) | collective-permute-done | bytes 1179680 | tf_op jit(solution)/shard_map/ppermute | solution.py:50
  276.5 18.6 %collective-permute-done.4 = bf16[512,1152]{1,0:T(8,128)(2,1)S(1)} collective-permute-done((bf16[512,1152]{1,0:T(8,128)(2,1)S(1)}, bf16[512,1152]{1,0:T(8,128)(2,1)S(1)}, u32[]{:S(2)}, u32[]{:S(2)}) %collective-permute-start.4) | collective-permute-done | bytes 1179680 | tf_op jit(solution)/shard_map/ppermute | solution.py:50
  300.7 25.8 %collective-permute-done.7 = bf16[512,1152]{1,0:T(8,128)(2,1)S(1)} collective-permute-done((bf16[512,1152]{1,0:T(8,128)(2,1)S(1)}, bf16[512,1152]{1,0:T(8,128)(2,1)S(1)}, u32[]{:S(2)}, u32[]{:S(2)}) %collective-permute-start.7) | collective-permute-done | bytes 1179680 | tf_op jit(solution)/shard_map/ppermute | solution.py:50
  331.0 10.7 %convolution_convert_fusion.1 = bf16[2304,1152]{0,1:T(8,128)(2,1)} fusion(bf16[1024,2304]{1,0:T(8,128)(2,1)} %get-tuple-element.258, bf16[512,1152]{1,0:T(8,128)(2,1)} %collective-permute-done.5, bf16[512,1152]{1,0:T(8,128)(2,1)} %get-tuple-element.232), kind=kOutput, calls=%fused_computation.44 | convolution fusion | flops 5443190784 | bytes 12386304 | tf_op jit(solution)/shard_map/dot_general | solution.py:26
  341.8 10.7 %convolution_convert_fusion = bf16[1152,2304]{1,0:T(8,128)(2,1)} fusion(bf16[1024,2304]{1,0:T(8,128)(2,1)} %get-tuple-element.263, bf16[512,1152]{1,0:T(8,128)(2,1)} %collective-permute-done.3, bf16[512,1152]{1,0:T(8,128)(2,1)} %add_convert_fusion.1), kind=kOutput, calls=%fused_computation.43 | convolution fusion | flops 5443190784 | bytes 12386304 | tf_op jit(solution)/shard_map/dot_general | solution.py:26
  365.0 116.9 %while.28 = (s32[]{:T(128)}, f32[8,1024,72]{1,2,0:T(8,128)}, f32[8,1024,72]{1,2,0:T(8,128)}, bf16[2,8,512,72]{2,3,1,0:T(8,128)(2,1)}, bf16[2,8,512,72]{2,3,1,0:T...) while((s32[]{:T(128)}, f32[8,1024,72]{1,2,0:T(8,128)}, ...), condition=%wide.region_12.13_spmd.clone, body=%wide.region_10.12_spmd.clone.sunk | while | flops 3073470464 | bytes 261996880 | solution.py:258
  373.5 10.4 %select_add_fusion.5 = f32[8,1024,72]{1,2,0:T(8,128)} fusion(f32[8,1024,72]{1,2,0:T(8,128)} %get-tuple-element.400, f32[8,512,1024]{2,1,0:T(8,128)} %fusion.162, f32[8,512]{1,0:T(8,128)S(1)} %dynamic-slice_bitcast_fusion.2, pred[]{:T(512)S(6)} %compare.4, bf16[2,8,512,72]{2,3,1,0:T(8,128)(2,1)} %get-tuple-element.416, s32[]{:T(128)S(6)} %copy.83), kind=kOutput, calls=%fused_computation.20.clone.1 | convolution fusion | flops 617742336 | bytes 22102020 | tf_op jit(solution)/shard_map/while/body/eval_jaxpr/hqk,hqd->hkd/dot_general | solution.py:249
  383.9 14.6 %multiply_reduce_fusion.11 = (f32[8,512]{1,0:T(8,128)S(1)}, f32[8,512,1024]{2,1,0:T(8,128)}) fusion(f32[8,512,1024]{2,1,0:T(8,128)} %fusion.162, f32[8,512]{1,0:T(8,128)S(1)} %dynamic-slice_bitcast_fusion.2, bf16[8,1024,72]{1,2,0:T(8,128)(2,1)} %get-tuple-element.417, bf16[2,8,512,72]{2,3,1,0:T(8,128)(2,1)} %get-tuple-element.416, s32[]{:T(128)S(6)} %copy.83), kind=kOutput, calls=%fused_computation.14.clone.1 | convolution fusion | flops 620752896 | bytes 35356676 | tf_op jit(solution)/shard_map/while/body/eval_jaxpr/hqd,hkd->hqk/dot_general | solution.py:233
  401.2 11.2 %multiply_convert_fusion.8 = bf16[8,512,1024]{2,1,0:T(8,128)(2,1)} fusion(f32[8,512,1024]{2,1,0:T(8,128)} %get-tuple-element.364, f32[8,512,1024]{2,1,0:T(8,128)S(1)} %copy-done.1, f32[8,512]{1,0:T(8,128)S(1)} %get-tuple-element.365, f32[8,512]{1,0:T(8,128)S(1)} %dynamic-slice_bitcast_fusion.2), kind=kLoop, calls=%fused_computation.13.clone.1 | loop fusion | flops 20971520 | bytes 41975808 | tf_op jit(solution)/shard_map/while/body/eval_jaxpr/convert_element_type | solution.py:237
  431.1 11.1 %select_add_fusion.5 = f32[8,1024,72]{1,2,0:T(8,128)} fusion(f32[8,1024,72]{1,2,0:T(8,128)} %get-tuple-element.400, f32[8,512,1024]{2,1,0:T(8,128)} %fusion.162, f32[8,512]{1,0:T(8,128)S(1)} %dynamic-slice_bitcast_fusion.2, pred[]{:T(512)S(6)} %compare.4, bf16[2,8,512,72]{2,3,1,0:T(8,128)(2,1)} %get-tuple-element.416, s32[]{:T(128)S(6)} %copy.83), kind=kOutput, calls=%fused_computation.20.clone.1 | convolution fusion | flops 617742336 | bytes 22102020 | tf_op jit(solution)/shard_map/while/body/eval_jaxpr/hqk,hqd->hkd/dot_general | solution.py:249
  442.2 14.6 %multiply_reduce_fusion.11 = (f32[8,512]{1,0:T(8,128)S(1)}, f32[8,512,1024]{2,1,0:T(8,128)}) fusion(f32[8,512,1024]{2,1,0:T(8,128)} %fusion.162, f32[8,512]{1,0:T(8,128)S(1)} %dynamic-slice_bitcast_fusion.2, bf16[8,1024,72]{1,2,0:T(8,128)(2,1)} %get-tuple-element.417, bf16[2,8,512,72]{2,3,1,0:T(8,128)(2,1)} %get-tuple-element.416, s32[]{:T(128)S(6)} %copy.83), kind=kOutput, calls=%fused_computation.14.clone.1 | convolution fusion | flops 620752896 | bytes 35356676 | tf_op jit(solution)/shard_map/while/body/eval_jaxpr/hqd,hkd->hqk/dot_general | solution.py:233
  459.2 10.5 %multiply_convert_fusion.8 = bf16[8,512,1024]{2,1,0:T(8,128)(2,1)} fusion(f32[8,512,1024]{2,1,0:T(8,128)} %get-tuple-element.364, f32[8,512,1024]{2,1,0:T(8,128)S(1)} %copy-done.1, f32[8,512]{1,0:T(8,128)S(1)} %get-tuple-element.365, f32[8,512]{1,0:T(8,128)S(1)} %dynamic-slice_bitcast_fusion.2), kind=kLoop, calls=%fused_computation.13.clone.1 | loop fusion | flops 20971520 | bytes 41975808 | tf_op jit(solution)/shard_map/while/body/eval_jaxpr/convert_element_type | solution.py:237
  488.0 65.6 %reduce-scatter.11.cloned.1.call-done = bf16[72,2304]{1,0:T(8,128)(2,1)} async-done(((bf16[1152,2304]{1,0:T(8,128)(2,1)}), bf16[72,2304]{1,0:T(8,128)(2,1)}) %reduce-scatter.11.cloned.1.call-update) | async-done | bytes 331792 | tf_op jit(solution)/shard_map/reduce_scatter | solution.py:80
  561.3 18.2 %copy.56 = bf16[1152,3,576]{2,1,0:T(4,128)(2,1)} copy(bf16[1152,3,576]{2,0,1:T(8,128)(2,1)S(1)} %convolution_convert_fusion.2) | data formatting | bytes 7962624
  579.5 12.3 %reshape.225 = bf16[1152,1728]{1,0:T(8,128)(2,1)} reshape(bf16[1152,3,576]{2,1,0:T(4,128)(2,1)} %copy.56) | data formatting | bytes 7962624
  603.7 21.7 %collective-permute-done.8 = bf16[512,1152]{1,0:T(8,128)(2,1)} collective-permute-done((bf16[512,1152]{1,0:T(8,128)(2,1)}, bf16[512,1152]{1,0:T(8,128)(2,1)}, u32[]{:S(2)}, u32[]{:S(2)}) %collective-permute-start.8) | collective-permute-done | bytes 1179680 | tf_op jit(solution)/shard_map/ppermute | solution.py:50
  636.3 11.1 %all_to_all.30 = f32[16,1,1008]{2,1,0:T(1,128)S(1)} all-to-all(f32[16,1,1008]{2,1,0:T(1,128)S(1)} %all_to_all.22), channel_id=1, replica_groups=mesh['fsdp'=16,'tp'=2] {'fsdp'}, dimensions={0} | all-to-all | bytes 129024 | tf_op jit(solution)/shard_map/all_to_all | solution.py:91
  (306 shorter events, 261.1 us)
Async XLA Ops:
  7.2 57.9 %all-gather.5.cloned.1.call-start = ((), (), s32[]{:S(2)}) async-start(), calls=%async_computation.7 | async-start | bytes 4700160 | tf_op jit(solution)/shard_map/all_gather | solution.py:123
  8.0 116.3 %all-gather.7.cloned.1.call-start = ((), (), s32[]{:S(2)}) async-start(), calls=%async_computation.8 | async-start | bytes 1566720 | tf_op jit(solution)/shard_map/all_gather | solution.py:124
  8.7 182.3 %all-gather.9.cloned.1.call-start = ((), (), s32[]{:S(2)}) async-start(), calls=%async_computation.9 | async-start | bytes 5640192 | tf_op jit(solution)/shard_map/all_gather | solution.py:125
  36.8 3.9 collective-permute-start
  41.4 10.7 %all-to-all-start = ((f32[16,1,432]{2,1,0:T(1,128)}), f32[16,1,432]{2,1,0:T(1,128)S(1)}, u32[]{:S(2)}, u32[]{:S(2)}) async-start(f32[16,1,432]{2,1,0:T(1,128)} %copy.43), calls=%async_computation | async-start | bytes 65536 | tf_op jit(solution)/shard_map/all_to_all | solution.py:91
  44.9 174.8 %all-gather.11.cloned.1.call-start = ((), (), s32[]{:S(2)}) async-start(), calls=%async_computation.10 | async-start | bytes 5640192 | tf_op jit(solution)/shard_map/all_gather | solution.py:126
  53.5 27.3 %collective-permute-start.1 = (bf16[512,1152]{1,0:T(8,128)(2,1)S(1)}, bf16[512,1152]{1,0:T(8,128)(2,1)S(1)}, u32[]{:S(2)}, u32[]{:S(2)}) collective-permute-start(bf16[512,1152]{1,0:T(8,128)(2,1)S(1)} %fusion.53), channel_id=1, source_target_pairs={{0,1},{1,0},{2,3},{3,2},{4,5},{5,4},{6,7},{7,6},{8,9},{9,8},{10,11... | collective-permute-start | bytes 3538952 | tf_op jit(solution)/shard_map/ppermute | solution.py:50
  55.0 433.0 %reduce-scatter.15.cloned.1.call-start = ((), (), s32[]{:S(2)}) async-start(), calls=%async_computation.14 | async-start | bytes 1566720
  128.0 26.7 %collective-permute-start.2 = (bf16[512,1152]{1,0:T(8,128)(2,1)}, bf16[512,1152]{1,0:T(8,128)(2,1)}, u32[]{:S(2)}, u32[]{:S(2)}) collective-permute-start(bf16[512,1152]{1,0:T(8,128)(2,1)} %convolution_convert_fusion.6), channel_id=1, source_target_pairs={{0,1},{1,0},{2,3},{3,2},{4,5},{5,4},{6,7},{7,6},{8,9},{9,8},{10,11... | collective-permute-start | bytes 3538952 | tf_op jit(solution)/shard_map/ppermute | solution.py:50
  161.8 29.2 %collective-permute-start.3 = (bf16[512,1152]{1,0:T(8,128)(2,1)}, bf16[512,1152]{1,0:T(8,128)(2,1)}, u32[]{:S(2)}, u32[]{:S(2)}) collective-permute-start(bf16[512,1152]{1,0:T(8,128)(2,1)} %add_convert_fusion.1), channel_id=1, source_target_pairs={{0,1},{1,0},{2,3},{3,2},{4,5},{5,4},{6,7},{7,6},{8,9},{9,8},{10,11... | collective-permute-start | bytes 3538952 | tf_op jit(solution)/shard_map/ppermute | solution.py:50
  167.5 45.3 %collective-permute-start.5 = (bf16[512,1152]{1,0:T(8,128)(2,1)}, bf16[512,1152]{1,0:T(8,128)(2,1)}, u32[]{:S(2)}, u32[]{:S(2)}) collective-permute-start(bf16[512,1152]{1,0:T(8,128)(2,1)} %get-tuple-element.232), channel_id=1, source_target_pairs={{0,1},{1,0},{2,3},{3,2},{4,5},{5,4},{6,7},{7,6},{8,9},{9,8},{10,11... | collective-permute-start | bytes 3538952 | tf_op jit(solution)/shard_map/ppermute | solution.py:50
  241.7 28.9 %collective-permute-start.6 = (bf16[512,1152]{1,0:T(8,128)(2,1)S(1)}, bf16[512,1152]{1,0:T(8,128)(2,1)S(1)}, u32[]{:S(2)}, u32[]{:S(2)}) collective-permute-start(bf16[512,1152]{1,0:T(8,128)(2,1)S(1)} %convolution_convert_fusion.4), channel_id=1, source_target_pairs={{0,1},{1,0},{2,3},{3,2},{4,5},{5,4},{6,7},{7,6},{8,9},{9,8},{10,11... | collective-permute-start | bytes 3538952 | tf_op jit(solution)/shard_map/ppermute | solution.py:50
  246.5 48.7 %collective-permute-start.4 = (bf16[512,1152]{1,0:T(8,128)(2,1)S(1)}, bf16[512,1152]{1,0:T(8,128)(2,1)S(1)}, u32[]{:S(2)}, u32[]{:S(2)}) collective-permute-start(bf16[512,1152]{1,0:T(8,128)(2,1)S(1)} %convolution_convert_fusion.5), channel_id=1, source_target_pairs={{0,1},{1,0},{2,3},{3,2},{4,5},{5,4},{6,7},{7,6},{8,9},{9,8},{10,11... | collective-permute-start | bytes 3538952 | tf_op jit(solution)/shard_map/ppermute | solution.py:50
  252.1 43.1 %copy-start.17 = (bf16[1,512,1152]{2,1,0:T(8,128)(2,1)S(1)}, bf16[1,512,1152]{2,1,0:T(8,128)(2,1)}, u32[]{:S(2)}) copy-start(bf16[1,512,1152]{2,1,0:T(8,128)(2,1)} %param.29) | copy-start | bytes 3538948
  295.2 32.5 %copy-start.19 = (bf16[2,8,9,8,512]{4,3,0,2,1:T(8,128)(2,1)S(1)}, bf16[2,8,9,8,512]{4,3,0,2,1:T(8,128)(2,1)}, u32[]{:S(2)}) copy-start(bf16[2,8,9,8,512]{4,3,0,2,1:T(8,128)(2,1)} %copy-done.18) | copy-start | bytes 3538948
  299.2 27.3 %collective-permute-start.7 = (bf16[512,1152]{1,0:T(8,128)(2,1)S(1)}, bf16[512,1152]{1,0:T(8,128)(2,1)S(1)}, u32[]{:S(2)}, u32[]{:S(2)}) collective-permute-start(bf16[512,1152]{1,0:T(8,128)(2,1)S(1)} %get-tuple-element.247), channel_id=1, source_target_pairs={{0,1},{1,0},{2,3},{3,2},{4,5},{5,4},{6,7},{7,6},{8,9},{9,8},{10,11... | collective-permute-start | bytes 3538952 | tf_op jit(solution)/shard_map/ppermute | solution.py:50
  331.0 157.0 %reduce-scatter.9.cloned.1.call-start = ((), (), s32[]{:S(2)}) async-start(), calls=%async_computation.11 | async-start | bytes 5640192 | tf_op jit(solution)/shard_map/reduce_scatter | solution.py:80
  341.7 211.9 %reduce-scatter.11.cloned.1.call-start = ((), (), s32[]{:S(2)}) async-start(), calls=%async_computation.12 | async-start | bytes 5640192 | tf_op jit(solution)/shard_map/reduce_scatter | solution.py:80
  352.5 311.5 %reduce-scatter.13.cloned.1.call-start = ((), (), s32[]{:S(2)}) async-start(), calls=%async_computation.13 | async-start | bytes 4386816
  485.7 67.9 %copy-start.24 = (bf16[512,1152]{1,0:T(8,128)(2,1)S(1)}, bf16[512,1152]{1,0:T(8,128)(2,1)}, u32[]{:S(2)}) copy-start(bf16[512,1152]{1,0:T(8,128)(2,1)} %copy-done.23) | copy-start | bytes 3538948
  485.7 67.9 %copy-start.56 = (bf16[512,1152]{1,0:T(8,128)(2,1)S(1)}, bf16[512,1152]{1,0:T(8,128)(2,1)}, u32[]{:S(2)}) copy-start(bf16[512,1152]{1,0:T(8,128)(2,1)} %copy-done.55) | copy-start | bytes 3538948
  598.6 26.7 %collective-permute-start.8 = (bf16[512,1152]{1,0:T(8,128)(2,1)}, bf16[512,1152]{1,0:T(8,128)(2,1)}, u32[]{:S(2)}, u32[]{:S(2)}) collective-permute-start(bf16[512,1152]{1,0:T(8,128)(2,1)} %fusion.43), channel_id=1, source_target_pairs={{0,1},{1,0},{2,3},{3,2},{4,5},{5,4},{6,7},{7,6},{8,9},{9,8},{10,11... | collective-permute-start | bytes 3538952 | tf_op jit(solution)/shard_map/ppermute | solution.py:50
  647.4 4.3 collective-permute-start.9
  652.8 10.4 %all-to-all-start.2 = ((f32[16,1,576]{2,1,0:T(1,128)}), f32[16,1,576]{2,1,0:T(1,128)S(1)}, u32[]{:S(2)}, u32[]{:S(2)}) async-start(f32[16,1,576]{2,1,0:T(1,128)} %copy.52), calls=%async_computation.4 | async-start | bytes 81920 | tf_op jit(solution)/shard_map/all_to_all | solution.py:91
  (64 other events, 795.6 us)
Sparse Core Ops, SparseCore 0:
  10.2 54.8 all-gather.4
  67.3 37.8 all-gather.6
  107.4 55.2 all-gather.8
  164.7 54.9 all-gather.10
  331.1 57.3 reduce-scatter.14
  392.4 78.4 reduce-scatter.8
  474.9 78.6 reduce-scatter.10
  591.9 71.8 reduce-scatter.12
where the time goes:
time: 677 us; the launch traced here: 673 us
  waiting for transfers between devices  243 us (36%)
  matrix products  223 us (33%)
  local copies, waits for them, and re-layouts  82.4 us (12%)
  other arithmetic  54.2 us (8%)
  blocking collectives  34.5 us (5%)
  starting transfers between devices  20.5 us (3%)
  between operations  15.1 us (2%)
    ppermute x10, waiting for transfers between devices, swap(): return lax.ppermute(values, 'tp', [(0, 1), (1, 0)])  149 us
    reduce_scatter x2, waiting for transfers between devices, reduce_grad(): lax.psum_scatter(term.astype(jnp.bfloat16), 'fsdp', scatter_dimension=axi...  65.6 us
    dot_general x6, matrix products, outer_cols(): lax.dot_general(left, right, (((1,), (1,)), ((), ())), preferred_element_...  46.6 us
    unnamed x110, local copies, waits for them, and re-layouts  40.1 us
    dot_general x6, matrix products, plain(): return jnp.dot(left, right, preferred_element_type=jnp.float32)  38.1 us
    dot_general x4, matrix products, inner_rows(): lax.dot_general(left, right, (((0,), (0,)), ((), ())), preferred_element_...  32.3 us
    dot_general x2, matrix products, attend_back(): jnp.einsum('hqd,hkd->hqk', grad_block, values_all, preferred_element_type...  29.2 us
    all_gather x1, blocking collectives, gather_small(): lax.all_gather(block, 'fsdp', axis=0, tiled=True).reshape(-1, padded)  23.3 us
  transfers between devices with their start and end apart: 20, of which 15 were waited for; matrix products, arithmetic and copies ran while one was open for 41% of the time, Pallas kernels for 0%

commit v1 on v0

--- a/solution.py
+++ b/solution.py
@@ -7,6 +7,27 @@
 HEAD_DIM = 72
 EPSILON = 1e-06
 HIGH = lax.Precision.HIGHEST
+
+
+def gather_around(value, axis, dim):
+    count, index, rows = (lax.axis_size(axis), lax.axis_index(axis), value.shape[dim])
+    right = [(i, (i + 1) % count) for i in range(count)]
+    left = [(i, (i - 1) % count) for i in range(count)]
+    out = jnp.zeros((*value.shape[:dim], count * rows, *value.shape[dim + 1 :]), value.dtype)
+    out = lax.dynamic_update_slice_in_dim(out, value, index * rows, axis=dim)
+    from_left = from_right = value
+    middle = count // 2
+    for step in range(1, middle + 1):
+        from_left = lax.ppermute(from_left, axis, right)
+        out = lax.dynamic_update_slice_in_dim(
+            out, from_left, (index - step) % count * rows, axis=dim
+        )
+        if step < count - middle:
+            from_right = lax.ppermute(from_right, axis, left)
+            out = lax.dynamic_update_slice_in_dim(
+                out, from_right, (index + step) % count * rows, axis=dim
+            )
+    return out
 
 
 def normalize(values):
@@ -84,7 +105,7 @@
     size = flat.shape[0]
     padded = -(-size // 1024) * 1024
     block = jnp.pad(flat, (0, padded - size)).reshape(8, padded // 8)
-    return lax.all_gather(block, "fsdp", axis=0, tiled=True).reshape(-1, padded)[:, :size]
+    return gather_around(block, "fsdp", 0).reshape(-1, padded)[:, :size]
 
 
 def trade(rows):

time: 677 us -> 696 us (1.028)
  starting transfers between devices: 20.5 us -> 53 us
  blocking collectives: 34.5 us -> 11.2 us
  waiting for transfers between devices: 243 us -> 250 us
    ppermute x0 -> x15, starting transfers between devices: none -> 32.4 us  [the longest x7 32.4 us: gather_around(): from_right = lax.ppermute(from_right, axis, left)]
    all_gather x1 -> x0, blocking collectives: 23.3 us -> none  [gather_small(): lax.all_gather(block, 'fsdp', axis=0, tiled=True).reshape(-1, padded)]
    ppermute x0 -> x15, waiting for transfers between devices: none -> 18 us  [the longest x8 11.5 us: gather_around(): from_left = lax.ppermute(from_left, axis, right)]
    all_gather x1, waiting for transfers between devices: 9.64 us -> 0.01 us  [shards(): qkv_full = lax.all_gather(qkv_weight, 'fsdp', axis=0, tiled=True)]
  transfers between devices with their start and end apart: 20 -> 35, of which waited for: 15 -> 20; matrix products, arithmetic and copies ran while one was open for 41% -> 40% of each run, Pallas kernels for 0% -> 0%
where the time goes in v1:
time: 696 us; the launch traced here: 691 us
  waiting for transfers between devices  250 us (36%)
  matrix products  223 us (32%)
  local copies, waits for them, and re-layouts  82.6 us (12%)
  other arithmetic  55.4 us (8%)
  starting transfers between devices  53 us (8%)
  between operations  15.4 us (2%)
  blocking collectives  11.2 us (2%)
    ppermute x10, waiting for transfers between devices, swap(): return lax.ppermute(values, 'tp', [(0, 1), (1, 0)])  153 us
    reduce_scatter x2, waiting for transfers between devices, reduce_grad(): lax.psum_scatter(term.astype(jnp.bfloat16), 'fsdp', scatter_dimension=axi...  67.8 us
    dot_general x6, matrix products, outer_cols(): lax.dot_general(left, right, (((1,), (1,)), ((), ())), preferred_element_...  46.6 us
    unnamed x110, local copies, waits for them, and re-layouts  40 us
    dot_general x6, matrix products, plain(): return jnp.dot(left, right, preferred_element_type=jnp.float32)  37.6 us
    ppermute x7, starting transfers between devices, gather_around(): from_right = lax.ppermute(from_right, axis, left)  32.4 us
    dot_general x4, matrix products, inner_rows(): lax.dot_general(left, right, (((0,), (0,)), ((), ())), preferred_element_...  32.4 us
    dot_general x2, matrix products, attend_back(): jnp.einsum('hqd,hkd->hqk', grad_block, values_all, preferred_element_type...  29.1 us
  transfers between devices with their start and end apart: 35, of which 20 were waited for; matrix products, arithmetic and copies ran while one was open for 40% of the time, Pallas kernels for 0%

profile of v1, /device:TPU:0, one launch (start us, length us, event | category | flops | bytes accessed | tf_op | source)
XLA Modules:
  0.0 690.9 jit_solution(7291762531083142735)
XLA Ops:
  91.0 18.5 %collective-permute-done.16 = bf16[512,1152]{1,0:T(8,128)(2,1)S(1)} collective-permute-done((bf16[512,1152]{1,0:T(8,128)(2,1)S(1)}, bf16[512,1152]{1,0:T(8,128)(2,1)S(1)}, u32[]{:S(2)}, u32[]{:S(2)}) %collective-permute-start.16) | collective-permute-done | bytes 1179680 | tf_op jit(solution)/shard_map/ppermute | solution.py:71
  125.6 23.9 %while.27 = (s32[]{:T(128)}, bf16[2,8,512,72]{2,3,1,0:T(8,128)(2,1)}, f32[2,8,512]{2,1,0:T(8,128)S(1)}, bf16[2,8,512,72]{2,3,1,0:T(8,128)(2,1)S(1)}, bf16[8,1024...) while((s32[]{:T(128)}, bf16[2,8,512,72]{2,3,1,0:T(8,128)(2,1)}, ...), condition=%wide.region_5.6_spmd, body=%wide.region_2.5_spmd.sunk | while | flops 1245704192 | bytes 68747440 | solution.py:207
  160.3 23.4 %collective-permute-done.17 = bf16[512,1152]{1,0:T(8,128)(2,1)} collective-permute-done((bf16[512,1152]{1,0:T(8,128)(2,1)}, bf16[512,1152]{1,0:T(8,128)(2,1)}, u32[]{:S(2)}, u32[]{:S(2)}) %collective-permute-start.17) | collective-permute-done | bytes 1179680 | tf_op jit(solution)/shard_map/ppermute | solution.py:71
  197.1 22.9 %collective-permute-done.18 = bf16[512,1152]{1,0:T(8,128)(2,1)} collective-permute-done((bf16[512,1152]{1,0:T(8,128)(2,1)}, bf16[512,1152]{1,0:T(8,128)(2,1)}, u32[]{:S(2)}, u32[]{:S(2)}) %collective-permute-start.18) | collective-permute-done | bytes 1179680 | tf_op jit(solution)/shard_map/ppermute | solution.py:71
  220.0 14.3 %multiply_convert_fusion.1 = (bf16[1024,2304]{1,0:T(8,128)(2,1)}, f32[1024,2304]{1,0:T(8,128)}) fusion(f32[2304]{0:T(1024)S(1)} %dynamic_slice.28, bf16[1152,2304]{1,0:T(8,128)(2,1)} %all-gather.9.cloned.1.call-done, bf16[512,1152]{1,0:T(8,128)(2,1)} %collective-permute-done.18, bf16[512,1152]{1,0:T(8,128)(2,1)} %add_convert_fusion.1), kind=kOutput, calls=%fused_computation.53 | convolution fusion | flops 5464129536 | bytes 21832704 | tf_op jit(solution)/shard_map/dot_general | solution.py:97
  242.2 17.1 %convert_reduce_fusion = (f32[2304]{0:T(1024)}, bf16[1024,2304]{1,0:T(8,128)(2,1)}) fusion(f32[1024,2304]{1,0:T(8,128)} %get-tuple-element.259, f32[2304]{0:T(1024)S(1)} %dynamic_slice.28, bf16[2304,1152]{0,1:T(8,128)(2,1)} %all-gather.11.cloned.1.call-done, bf16[512,1152]{1,0:T(8,128)(2,1)} %collective-permute-done.20, ...), kind=kOutput, calls=%fused_computation.52 | convolution fusion | flops 5494798336 | bytes 21841920 | tf_op jit(solution)/shard_map/dot_general | solution.py:53
  274.7 18.6 %collective-permute-done.21 = bf16[512,1152]{1,0:T(8,128)(2,1)S(1)} collective-permute-done((bf16[512,1152]{1,0:T(8,128)(2,1)S(1)}, bf16[512,1152]{1,0:T(8,128)(2,1)S(1)}, u32[]{:S(2)}, u32[]{:S(2)}) %collective-permute-start.21) | collective-permute-done | bytes 1179680 | tf_op jit(solution)/shard_map/ppermute | solution.py:71
  299.3 15.3 %collective-permute-done.19 = bf16[512,1152]{1,0:T(8,128)(2,1)S(1)} collective-permute-done((bf16[512,1152]{1,0:T(8,128)(2,1)S(1)}, bf16[512,1152]{1,0:T(8,128)(2,1)S(1)}, u32[]{:S(2)}, u32[]{:S(2)}) %collective-permute-start.19) | collective-permute-done | bytes 1179680 | tf_op jit(solution)/shard_map/ppermute | solution.py:71
  320.1 22.5 %collective-permute-done.22 = bf16[512,1152]{1,0:T(8,128)(2,1)S(1)} collective-permute-done((bf16[512,1152]{1,0:T(8,128)(2,1)S(1)}, bf16[512,1152]{1,0:T(8,128)(2,1)S(1)}, u32[]{:S(2)}, u32[]{:S(2)}) %collective-permute-start.22) | collective-permute-done | bytes 1179680 | tf_op jit(solution)/shard_map/ppermute | solution.py:71
  347.0 10.9 %convolution_convert_fusion.1 = bf16[2304,1152]{0,1:T(8,128)(2,1)} fusion(bf16[1024,2304]{1,0:T(8,128)(2,1)} %get-tuple-element.258, bf16[512,1152]{1,0:T(8,128)(2,1)} %collective-permute-done.20, bf16[512,1152]{1,0:T(8,128)(2,1)} %get-tuple-element.232), kind=kOutput, calls=%fused_computation.44 | convolution fusion | flops 5443190784 | bytes 12386304 | tf_op jit(solution)/shard_map/dot_general | solution.py:47
  358.0 10.5 %convolution_convert_fusion = bf16[1152,2304]{1,0:T(8,128)(2,1)} fusion(bf16[1024,2304]{1,0:T(8,128)(2,1)} %get-tuple-element.263, bf16[512,1152]{1,0:T(8,128)(2,1)} %collective-permute-done.18, bf16[512,1152]{1,0:T(8,128)(2,1)} %add_convert_fusion.1), kind=kOutput, calls=%fused_computation.43 | convolution fusion | flops 5443190784 | bytes 12386304 | tf_op jit(solution)/shard_map/dot_general | solution.py:47
  381.0 116.6 %while.28 = (s32[]{:T(128)}, f32[8,1024,72]{1,2,0:T(8,128)}, f32[8,1024,72]{1,2,0:T(8,128)}, bf16[2,8,512,72]{2,3,1,0:T(8,128)(2,1)}, bf16[2,8,512,72]{2,3,1,0:T...) while((s32[]{:T(128)}, f32[8,1024,72]{1,2,0:T(8,128)}, ...), condition=%wide.region_12.13_spmd.clone, body=%wide.region_10.12_spmd.clone.sunk | while | flops 3073470464 | bytes 261996880 | solution.py:279
  381.2 8.1 %fusion.163 = f32[8,512,1024]{2,1,0:T(8,128)} fusion(bf16[8,1024,72]{1,2,0:T(8,128)(2,1)S(1)} %get-tuple-element.414, bf16[2,8,512,72]{2,3,1,0:T(8,128)(2,1)S(1)} %get-tuple-element.413, s32[]{:T(128)S(6)} %copy.99), kind=kOutput, calls=%fused_computation.29.clone.1 | convolution fusion | flops 603979776 | bytes 18546692 | tf_op jit(solution)/shard_map/while/body/eval_jaxpr/hqd,hkd->hqk/dot_general | solution.py:250
  389.4 10.4 %select_add_fusion.5 = f32[8,1024,72]{1,2,0:T(8,128)} fusion(f32[8,1024,72]{1,2,0:T(8,128)} %get-tuple-element.400, f32[8,512,1024]{2,1,0:T(8,128)} %fusion.163, f32[8,512]{1,0:T(8,128)S(1)} %dynamic-slice_bitcast_fusion.2, pred[]{:T(512)S(6)} %compare.19, bf16[2,8,512,72]{2,3,1,0:T(8,128)(2,1)} %get-tuple-element.416, s32[]{:T(128)S(6)} %copy.99), kind=kOutput, calls=%fused_computation.20.clone.1 | convolution fusion | flops 617742336 | bytes 22102020 | tf_op jit(solution)/shard_map/while/body/eval_jaxpr/hqk,hqd->hkd/dot_general | solution.py:270
  399.8 14.6 %multiply_reduce_fusion.11 = (f32[8,512]{1,0:T(8,128)S(1)}, f32[8,512,1024]{2,1,0:T(8,128)}) fusion(f32[8,512,1024]{2,1,0:T(8,128)} %fusion.163, f32[8,512]{1,0:T(8,128)S(1)} %dynamic-slice_bitcast_fusion.2, bf16[8,1024,72]{1,2,0:T(8,128)(2,1)} %get-tuple-element.417, bf16[2,8,512,72]{2,3,1,0:T(8,128)(2,1)} %get-tuple-element.416, s32[]{:T(128)S(6)} %copy.99), kind=kOutput, calls=%fused_computation.14.clone.1 | convolution fusion | flops 620752896 | bytes 35356676 | tf_op jit(solution)/shard_map/while/body/eval_jaxpr/hqd,hkd->hqk/dot_general | solution.py:254
  416.8 11.2 %multiply_convert_fusion.8 = bf16[8,512,1024]{2,1,0:T(8,128)(2,1)} fusion(f32[8,512,1024]{2,1,0:T(8,128)} %get-tuple-element.364, f32[8,512,1024]{2,1,0:T(8,128)S(1)} %copy-done.1, f32[8,512]{1,0:T(8,128)S(1)} %get-tuple-element.365, f32[8,512]{1,0:T(8,128)S(1)} %dynamic-slice_bitcast_fusion.2), kind=kLoop, calls=%fused_computation.13.clone.1 | loop fusion | flops 20971520 | bytes 41975808 | tf_op jit(solution)/shard_map/while/body/eval_jaxpr/convert_element_type | solution.py:258
  446.8 11.1 %select_add_fusion.5 = f32[8,1024,72]{1,2,0:T(8,128)} fusion(f32[8,1024,72]{1,2,0:T(8,128)} %get-tuple-element.400, f32[8,512,1024]{2,1,0:T(8,128)} %fusion.163, f32[8,512]{1,0:T(8,128)S(1)} %dynamic-slice_bitcast_fusion.2, pred[]{:T(512)S(6)} %compare.19, bf16[2,8,512,72]{2,3,1,0:T(8,128)(2,1)} %get-tuple-element.416, s32[]{:T(128)S(6)} %copy.99), kind=kOutput, calls=%fused_computation.20.clone.1 | convolution fusion | flops 617742336 | bytes 22102020 | tf_op jit(solution)/shard_map/while/body/eval_jaxpr/hqk,hqd->hkd/dot_general | solution.py:270
  457.9 14.6 %multiply_reduce_fusion.11 = (f32[8,512]{1,0:T(8,128)S(1)}, f32[8,512,1024]{2,1,0:T(8,128)}) fusion(f32[8,512,1024]{2,1,0:T(8,128)} %fusion.163, f32[8,512]{1,0:T(8,128)S(1)} %dynamic-slice_bitcast_fusion.2, bf16[8,1024,72]{1,2,0:T(8,128)(2,1)} %get-tuple-element.417, bf16[2,8,512,72]{2,3,1,0:T(8,128)(2,1)} %get-tuple-element.416, s32[]{:T(128)S(6)} %copy.99), kind=kOutput, calls=%fused_computation.14.clone.1 | convolution fusion | flops 620752896 | bytes 35356676 | tf_op jit(solution)/shard_map/while/body/eval_jaxpr/hqd,hkd->hqk/dot_general | solution.py:254
  475.0 10.4 %multiply_convert_fusion.8 = bf16[8,512,1024]{2,1,0:T(8,128)(2,1)} fusion(f32[8,512,1024]{2,1,0:T(8,128)} %get-tuple-element.364, f32[8,512,1024]{2,1,0:T(8,128)S(1)} %copy-done.1, f32[8,512]{1,0:T(8,128)S(1)} %get-tuple-element.365, f32[8,512]{1,0:T(8,128)S(1)} %dynamic-slice_bitcast_fusion.2), kind=kLoop, calls=%fused_computation.13.clone.1 | loop fusion | flops 20971520 | bytes 41975808 | tf_op jit(solution)/shard_map/while/body/eval_jaxpr/convert_element_type | solution.py:258
  503.7 67.8 %reduce-scatter.11.cloned.1.call-done = bf16[72,2304]{1,0:T(8,128)(2,1)} async-done(((bf16[1152,2304]{1,0:T(8,128)(2,1)}), bf16[72,2304]{1,0:T(8,128)(2,1)}) %reduce-scatter.11.cloned.1.call-update) | async-done | bytes 331792 | tf_op jit(solution)/shard_map/reduce_scatter | solution.py:101
  579.1 18.2 %copy.56 = bf16[1152,3,576]{2,1,0:T(4,128)(2,1)} copy(bf16[1152,3,576]{2,0,1:T(8,128)(2,1)S(1)} %convolution_convert_fusion.2) | data formatting | bytes 7962624
  597.3 12.3 %reshape.225 = bf16[1152,1728]{1,0:T(8,128)(2,1)} reshape(bf16[1152,3,576]{2,1,0:T(4,128)(2,1)} %copy.56) | data formatting | bytes 7962624
  621.8 21.3 %collective-permute-done.23 = bf16[512,1152]{1,0:T(8,128)(2,1)} collective-permute-done((bf16[512,1152]{1,0:T(8,128)(2,1)}, bf16[512,1152]{1,0:T(8,128)(2,1)}, u32[]{:S(2)}, u32[]{:S(2)}) %collective-permute-start.23) | collective-permute-done | bytes 1179680 | tf_op jit(solution)/shard_map/ppermute | solution.py:71
  654.1 11.2 %all_to_all.30 = f32[16,1,1008]{2,1,0:T(1,128)S(1)} all-to-all(f32[16,1,1008]{2,1,0:T(1,128)S(1)} %all_to_all.22), channel_id=1, replica_groups=mesh['fsdp'=16,'tp'=2] {'fsdp'}, dimensions={0} | all-to-all | bytes 129024 | tf_op jit(solution)/shard_map/all_to_all | solution.py:112
  (352 shorter events, 290.0 us)
Async XLA Ops:
  7.2 76.7 %all-gather.5.cloned.1.call-start = ((), (), s32[]{:S(2)}) async-start(), calls=%async_computation.7 | async-start | bytes 4700160 | tf_op jit(solution)/shard_map/all_gather | solution.py:144
  8.0 145.0 %all-gather.7.cloned.1.call-start = ((), (), s32[]{:S(2)}) async-start(), calls=%async_computation.8 | async-start | bytes 1566720 | tf_op jit(solution)/shard_map/all_gather | solution.py:145
  8.7 211.3 %all-gather.9.cloned.1.call-start = ((), (), s32[]{:S(2)}) async-start(), calls=%async_computation.9 | async-start | bytes 5640192 | tf_op jit(solution)/shard_map/all_gather | solution.py:146
  13.0 7.2 %collective-permute-start.1 = (bf16[8,256]{1,0:T(8,128)(2,1)S(1)}, bf16[8,256]{1,0:T(8,128)(2,1)S(1)}, u32[]{:S(2)}, u32[]{:S(2)}) collective-permute-start(bf16[8,256]{1,0:T(8,128)(2,1)S(1)} %reshape.202), channel_id=1, source_target_pairs={{0,30},{2,0},{4,2},{6,4},{8,6},{10,8},{12,10},{14,12},{16,14},{18,... | collective-permute-start | bytes 12296 | tf_op jit(solution)/shard_map/ppermute | solution.py:26
  18.5 6.2 collective-permute-start
  42.0 5.9 collective-permute-start.8
  43.3 5.9 collective-permute-start.11
  47.9 5.9 collective-permute-start.10
  49.2 10.3 %collective-permute-start.13 = (bf16[8,256]{1,0:T(8,128)(2,1)S(1)}, bf16[8,256]{1,0:T(8,128)(2,1)S(1)}, u32[]{:S(2)}, u32[]{:S(2)}) collective-permute-start(bf16[8,256]{1,0:T(8,128)(2,1)S(1)} %collective-permute-done.11), channel_id=1, source_target_pairs={{0,30},{2,0},{4,2},{6,4},{8,6},{10,8},{12,10},{14,12},{16,14},{18,... | collective-permute-start | bytes 12296 | tf_op jit(solution)/shard_map/ppermute | solution.py:26
  70.2 10.3 %all-to-all-start = ((f32[16,1,432]{2,1,0:T(1,128)}), f32[16,1,432]{2,1,0:T(1,128)S(1)}, u32[]{:S(2)}, u32[]{:S(2)}) async-start(f32[16,1,432]{2,1,0:T(1,128)} %copy.43), calls=%async_computation | async-start | bytes 65536 | tf_op jit(solution)/shard_map/all_to_all | solution.py:112
  73.7 168.5 %all-gather.11.cloned.1.call-start = ((), (), s32[]{:S(2)}) async-start(), calls=%async_computation.10 | async-start | bytes 5640192 | tf_op jit(solution)/shard_map/all_gather | solution.py:147
  81.9 27.5 %collective-permute-start.16 = (bf16[512,1152]{1,0:T(8,128)(2,1)S(1)}, bf16[512,1152]{1,0:T(8,128)(2,1)S(1)}, u32[]{:S(2)}, u32[]{:S(2)}) collective-permute-start(bf16[512,1152]{1,0:T(8,128)(2,1)S(1)} %fusion.53), channel_id=1, source_target_pairs={{0,1},{1,0},{2,3},{3,2},{4,5},{5,4},{6,7},{7,6},{8,9},{9,8},{10,11... | collective-permute-start | bytes 3538952 | tf_op jit(solution)/shard_map/ppermute | solution.py:71
  83.4 420.3 %reduce-scatter.15.cloned.1.call-start = ((), (), s32[]{:S(2)}) async-start(), calls=%async_computation.14 | async-start | bytes 1566720
  156.7 27.0 %collective-permute-start.17 = (bf16[512,1152]{1,0:T(8,128)(2,1)}, bf16[512,1152]{1,0:T(8,128)(2,1)}, u32[]{:S(2)}, u32[]{:S(2)}) collective-permute-start(bf16[512,1152]{1,0:T(8,128)(2,1)} %convolution_convert_fusion.6), channel_id=1, source_target_pairs={{0,1},{1,0},{2,3},{3,2},{4,5},{5,4},{6,7},{7,6},{8,9},{9,8},{10,11... | collective-permute-start | bytes 3538952 | tf_op jit(solution)/shard_map/ppermute | solution.py:71
  190.8 29.2 %collective-permute-start.18 = (bf16[512,1152]{1,0:T(8,128)(2,1)}, bf16[512,1152]{1,0:T(8,128)(2,1)}, u32[]{:S(2)}, u32[]{:S(2)}) collective-permute-start(bf16[512,1152]{1,0:T(8,128)(2,1)} %add_convert_fusion.1), channel_id=1, source_target_pairs={{0,1},{1,0},{2,3},{3,2},{4,5},{5,4},{6,7},{7,6},{8,9},{9,8},{10,11... | collective-permute-start | bytes 3538952 | tf_op jit(solution)/shard_map/ppermute | solution.py:71
  196.5 45.7 %collective-permute-start.20 = (bf16[512,1152]{1,0:T(8,128)(2,1)}, bf16[512,1152]{1,0:T(8,128)(2,1)}, u32[]{:S(2)}, u32[]{:S(2)}) collective-permute-start(bf16[512,1152]{1,0:T(8,128)(2,1)} %get-tuple-element.232), channel_id=1, source_target_pairs={{0,1},{1,0},{2,3},{3,2},{4,5},{5,4},{6,7},{7,6},{8,9},{9,8},{10,11... | collective-permute-start | bytes 3538952 | tf_op jit(solution)/shard_map/ppermute | solution.py:71
  264.4 29.0 %collective-permute-start.21 = (bf16[512,1152]{1,0:T(8,128)(2,1)S(1)}, bf16[512,1152]{1,0:T(8,128)(2,1)S(1)}, u32[]{:S(2)}, u32[]{:S(2)}) collective-permute-start(bf16[512,1152]{1,0:T(8,128)(2,1)S(1)} %convolution_convert_fusion.4), channel_id=1, source_target_pairs={{0,1},{1,0},{2,3},{3,2},{4,5},{5,4},{6,7},{7,6},{8,9},{9,8},{10,11... | collective-permute-start | bytes 3538952 | tf_op jit(solution)/shard_map/ppermute | solution.py:71
  269.1 45.5 %collective-permute-start.19 = (bf16[512,1152]{1,0:T(8,128)(2,1)S(1)}, bf16[512,1152]{1,0:T(8,128)(2,1)S(1)}, u32[]{:S(2)}, u32[]{:S(2)}) collective-permute-start(bf16[512,1152]{1,0:T(8,128)(2,1)S(1)} %convolution_convert_fusion.5), channel_id=1, source_target_pairs={{0,1},{1,0},{2,3},{3,2},{4,5},{5,4},{6,7},{7,6},{8,9},{9,8},{10,11... | collective-permute-start | bytes 3538952 | tf_op jit(solution)/shard_map/ppermute | solution.py:71
  318.6 24.0 %collective-permute-start.22 = (bf16[512,1152]{1,0:T(8,128)(2,1)S(1)}, bf16[512,1152]{1,0:T(8,128)(2,1)S(1)}, u32[]{:S(2)}, u32[]{:S(2)}) collective-permute-start(bf16[512,1152]{1,0:T(8,128)(2,1)S(1)} %get-tuple-element.247), channel_id=1, source_target_pairs={{0,1},{1,0},{2,3},{3,2},{4,5},{5,4},{6,7},{7,6},{8,9},{9,8},{10,11... | collective-permute-start | bytes 3538952 | tf_op jit(solution)/shard_map/ppermute | solution.py:71
  346.9 156.7 %reduce-scatter.9.cloned.1.call-start = ((), (), s32[]{:S(2)}) async-start(), calls=%async_computation.11 | async-start | bytes 5640192 | tf_op jit(solution)/shard_map/reduce_scatter | solution.py:101
  357.9 213.5 %reduce-scatter.11.cloned.1.call-start = ((), (), s32[]{:S(2)}) async-start(), calls=%async_computation.12 | async-start | bytes 5640192 | tf_op jit(solution)/shard_map/reduce_scatter | solution.py:101
  368.6 313.2 %reduce-scatter.13.cloned.1.call-start = ((), (), s32[]{:S(2)}) async-start(), calls=%async_computation.13 | async-start | bytes 4386816
  616.4 26.7 %collective-permute-start.23 = (bf16[512,1152]{1,0:T(8,128)(2,1)}, bf16[512,1152]{1,0:T(8,128)(2,1)}, u32[]{:S(2)}, u32[]{:S(2)}) collective-permute-start(bf16[512,1152]{1,0:T(8,128)(2,1)} %fusion.43), channel_id=1, source_target_pairs={{0,1},{1,0},{2,3},{3,2},{4,5},{5,4},{6,7},{7,6},{8,9},{9,8},{10,11... | collective-permute-start | bytes 3538952 | tf_op jit(solution)/shard_map/ppermute | solution.py:71
  670.7 10.4 %all-to-all-start.2 = ((f32[16,1,576]{2,1,0:T(1,128)}), f32[16,1,576]{2,1,0:T(1,128)S(1)}, u32[]{:S(2)}, u32[]{:S(2)}) async-start(f32[16,1,576]{2,1,0:T(1,128)} %copy.52), calls=%async_computation.4 | async-start | bytes 81920 | tf_op jit(solution)/shard_map/all_to_all | solution.py:112
  (79 other events, 1197.2 us)
Sparse Core Ops, SparseCore 0:
  10.2 54.6 all-gather.4
  67.1 38.5 all-gather.6
  107.9 55.1 all-gather.8
  165.2 54.9 all-gather.10
  347.1 59.3 reduce-scatter.14
  410.3 78.4 reduce-scatter.8
  492.8 78.5 reduce-scatter.10
  609.7 71.9 reduce-scatter.12
